TPU v7x, 512 devices: a whole 4x8x8 slice. The times are simulated.
512 devices in a mesh: dp: 128 (over y, z, core), mp: 4 (over x).
Axes of the slice: x: 4, y: 8, z: 8, core: 2. Of those that a mesh axis runs over, the one named last changes fastest.
Arguments:
- query_hidden: bfloat16 [4096, 32, 768], P('dp', None, 'mp'), may hold values from -6 to 6
- query_proj: bfloat16 [768, 128], P('mp'), may hold values from -0.21875 to 0.21875
- passages: bfloat16 [8192, 128, 128], P(('dp', 'mp')), may hold values from -6 to 6
- teacher: float32 [4096, 4, 64], P('dp'), may hold values from -8 to 8
- neg_blocks: int32 [4096, 4], P('dp'), may hold values from 0 to 127, all different within a row; in each aligned block of 32 rows (0 to 31, 32 to 63, ...) at most 2 rows name the same one
Outputs:
- kl_loss: float32 [4096], P('dp')
Inputs may be any that keep to these rules, and one draw needn't show every extreme that they name: `neg_blocks`: each query names 4 different blocks. Among the 32 queries of one dp index no block is named more than 2 times, and some block is named exactly 2 times.
All inputs are finite; a program needn't handle non-finite values.
Results may differ from a plain program's by a relative error of at most 0.0003.
Values may be sent and summed in bfloat16 or wider, within the bound.
No kernel may reach another device: no remote copies, remote signals or barrier semaphores. Data moves between devices by JAX's collectives and lax.ppermute only.
A program may use at most 64 MiB of HBM per device.

v0:
```python
import jax
import jax.numpy as jnp
from jax import lax
from jax.sharding import PartitionSpec as P

softness = 0.1


def unit_rows(values):
    return values * lax.rsqrt(jnp.sum(values * values, axis=-1, keepdims=True) + 1e-06)


def soft_scores(slot_rows, passage_vecs):
    slot_count = slot_rows.shape[0]
    block_size = 16
    padded_count = -(-slot_count // block_size) * block_size
    blocked = slot_rows.reshape(
        padded_count // block_size, block_size, slot_rows.shape[1], slot_rows.shape[2]
    )

    def block_scores(slot_block):
        sims = jnp.einsum(
            "sie,pje->sipj", slot_block, passage_vecs, preferred_element_type=jnp.float32
        )
        softened = softness * jnp.log(jnp.sum(jnp.exp(sims / softness), axis=-1))
        return jnp.sum(softened, axis=1)

    scored = lax.map(block_scores, blocked)
    return scored.reshape(padded_count, -1)


def per_device(query_hidden, query_proj, passages, teacher, neg_blocks):
    partial_sum = jnp.einsum(
        "qth,he->qte", query_hidden, query_proj, preferred_element_type=jnp.float32
    )
    passage_vecs = unit_rows(passages.astype(jnp.float32)).astype(jnp.bfloat16)
    dp_count = lax.axis_size("dp")
    query_count, pick_count = neg_blocks.shape
    embed_width = partial_sum.shape[2]
    row_count = query_count * pick_count
    capacity = max(2, -(-row_count // dp_count))
    slots_all = dp_count * capacity
    owners = neg_blocks.reshape(row_count)
    owner_hits = (owners[:, None] == jnp.arange(dp_count, dtype=jnp.int32)[None, :]).astype(
        jnp.int32
    )
    earlier = jnp.cumsum(owner_hits, axis=0) - owner_hits
    slot_rank = jnp.sum(earlier * owner_hits, axis=1)
    slot_ids = owners * capacity + slot_rank
    matches = (slot_ids[None, :] == jnp.arange(slots_all, dtype=jnp.int32)[:, None]).astype(
        jnp.int32
    )
    row_query = jnp.arange(row_count, dtype=jnp.int32) // pick_count
    source = jnp.sum(matches * row_query[None, :], axis=1)
    filled = jnp.sum(matches, axis=1)
    projected = lax.psum(partial_sum, "mp")
    query_vecs = unit_rows(projected).astype(jnp.bfloat16)
    tokens = query_vecs.shape[1]
    outgoing = query_vecs[source] * filled[:, None, None].astype(jnp.bfloat16)
    outgoing = outgoing.reshape(dp_count, capacity, tokens, embed_width)
    arrived_items = lax.all_to_all(outgoing, "dp", split_axis=0, concat_axis=0, tiled=True)
    dims_items = arrived_items.shape
    flat_items = arrived_items.reshape(dims_items[0] * dims_items[1], dims_items[2], dims_items[3])
    scores = soft_scores(flat_items, passage_vecs).reshape(dims_items[0], dims_items[1], -1)
    returned = lax.all_to_all(scores, "dp", split_axis=0, concat_axis=0, tiled=True)
    home_scores = returned.reshape(slots_all, -1)[slot_ids].reshape(query_count, pick_count, -1)
    teacher_logp = teacher - jnp.log(jnp.sum(jnp.exp(teacher), axis=(1, 2), keepdims=True))
    student = lax.all_gather(home_scores, "mp", axis=2, tiled=True)
    kl_loss = jnp.sum(jnp.exp(teacher_logp) * (teacher_logp - student), axis=(1, 2)) + jnp.log(
        jnp.sum(jnp.exp(student), axis=(1, 2))
    )
    return kl_loss


def solution(mesh):
    in_specs = (
        P("dp", None, "mp"),
        P("mp", None),
        P(("dp", "mp"), None, None),
        P("dp", None, None),
        P("dp", None),
    )
    out_specs = P("dp")
    return jax.shard_map(
        per_device, mesh=mesh, in_specs=in_specs, out_specs=out_specs, check_vma=False
    )
```

profile of v0, /device:TPU:8, one launch (start us, length us, event | category | flops | bytes accessed | tf_op | source)
XLA Modules:
  0.0 229.7 jit_solution(16609151651576874862)
XLA Ops:
  6.5 1.0 copy-done
  7.6 1.9 fusion.7
  9.5 0.8 copy.19
  10.5 0.2 reduce_window_sum.11
  10.6 0.2 select_reduce_fusion.1
  10.8 0.2 convert_reduce_fusion
  11.0 0.2 convert_element_type.30
  11.2 57.0 %all-reduce.2.cloned.1.call-done = f32[32,32,128]{2,1,0:T(8,128)} async-done(((f32[32,32,128]{2,1,0:T(8,128)}), f32[32,32,128]{2,1,0:T(8,128)}) %all-reduce.2.cloned.1.call-update) | async-done | bytes 524304 | tf_op jit(solution)/shard_map/psum | solution.py:56
  68.2 1.2 multiply_reduce_fusion.1
  69.4 1.2 multiply_convert_fusion
  70.7 1.0 gather_fusion
  71.7 1.7 broadcast_multiply_fusion
  73.4 14.3 %all-to-all-start = ((bf16[128,2,32,128]{3,2,1,0:T(8,128)(2,1)}), bf16[128,2,32,128]{3,2,1,0:T(8,128)(2,1)S(1)}, u32[]{:S(2)}, u32[]{:S(2)}) async-start(bf16[128,2,32,128]{3,2,1,0:T(8,128)(2,1)} %broadcast_multiply_fusion), calls=%async_computation | async-start | bytes 4194304 | tf_op jit(solution)/shard_map/all_to_all | solution.py:61
  87.9 0.3 exponential_reduce_fusion.2
  88.2 0.3 fusion.4
  88.6 1.1 fusion.5
  89.8 50.3 %all-to-all-done = bf16[128,2,32,128]{3,2,1,0:T(8,128)(2,1)S(1)} async-done(((bf16[128,2,32,128]{3,2,1,0:T(8,128)(2,1)}), bf16[128,2,32,128]{3,2,1,0:T(8,128)(2,1)S(1)}, u32[]{:S(2)}, u32[]{:S(2)}) %all-to-all-start) | async-done | bytes 2097184 | tf_op jit(solution)/shard_map/all_to_all | solution.py:61
  140.1 49.7 %while.10 = (s32[]{:T(128)}, f32[16,16,16]{2,1,0:T(8,128)}, bf16[16,16,32,128]{3,2,1,0:T(8,128)(2,1)S(1)}, bf16[16,128,128]{2,1,0:T(8,128)(2,1)}, s32[]{:T(128)}) while((s32[]{:T(128)}, f32[16,16,16]{2,1,0:T(8,128)}, bf16[16,16,32,128]{3,2,1,0:T(8,128)(2,1)S(1)}, bf16[16,128,128]{2,1,0:T(8,128)(2,1)}, s32[]{:T(128)}) %tuple.25), condition=%wide.region_11.12_spmd, body=%wide.region_8.11_spmd.sunk | while | flops 270540544 | bytes 731713 | solution.py:28
  140.1 2.4 %exponential_reduce_fusion.4 = f32[16,32,16]{1,2,0:T(8,128)S(1)} fusion(bf16[16,128,128]{2,1,0:T(8,128)(2,1)} %get-tuple-element.78, bf16[16,16,32,128]{3,2,1,0:T(8,128)(2,1)S(1)} %get-tuple-element.77, s32[]{:T(128)} %get-tuple-element.70), kind=kOutput, calls=%fused_computation.2.clone.1 | convolution fusion | flops 270524416 | bytes 688132 | tf_op jit(solution)/shard_map/while/body/eval_jaxpr/sie,pje->sipj/dot_general | solution.py:22
  142.4 0.1 multiply_reduce_fusion.4
  142.6 0.6 bitcast_dynamic-update-slice_fusion.2
  143.2 2.4 %exponential_reduce_fusion.4 = f32[16,32,16]{1,2,0:T(8,128)S(1)} fusion(bf16[16,128,128]{2,1,0:T(8,128)(2,1)} %get-tuple-element.78, bf16[16,16,32,128]{3,2,1,0:T(8,128)(2,1)S(1)} %get-tuple-element.77, s32[]{:T(128)} %get-tuple-element.70), kind=kOutput, calls=%fused_computation.2.clone.1 | convolution fusion | flops 270524416 | bytes 688132 | tf_op jit(solution)/shard_map/while/body/eval_jaxpr/sie,pje->sipj/dot_general | solution.py:22
  145.5 0.1 multiply_reduce_fusion.4
  145.7 0.6 bitcast_dynamic-update-slice_fusion.2
  146.3 2.4 %exponential_reduce_fusion.4 = f32[16,32,16]{1,2,0:T(8,128)S(1)} fusion(bf16[16,128,128]{2,1,0:T(8,128)(2,1)} %get-tuple-element.78, bf16[16,16,32,128]{3,2,1,0:T(8,128)(2,1)S(1)} %get-tuple-element.77, s32[]{:T(128)} %get-tuple-element.70), kind=kOutput, calls=%fused_computation.2.clone.1 | convolution fusion | flops 270524416 | bytes 688132 | tf_op jit(solution)/shard_map/while/body/eval_jaxpr/sie,pje->sipj/dot_general | solution.py:22
  148.7 0.1 multiply_reduce_fusion.4
  148.8 0.6 bitcast_dynamic-update-slice_fusion.2
  149.4 2.4 %exponential_reduce_fusion.4 = f32[16,32,16]{1,2,0:T(8,128)S(1)} fusion(bf16[16,128,128]{2,1,0:T(8,128)(2,1)} %get-tuple-element.78, bf16[16,16,32,128]{3,2,1,0:T(8,128)(2,1)S(1)} %get-tuple-element.77, s32[]{:T(128)} %get-tuple-element.70), kind=kOutput, calls=%fused_computation.2.clone.1 | convolution fusion | flops 270524416 | bytes 688132 | tf_op jit(solution)/shard_map/while/body/eval_jaxpr/sie,pje->sipj/dot_general | solution.py:22
  151.8 0.1 multiply_reduce_fusion.4
  151.9 0.6 bitcast_dynamic-update-slice_fusion.2
  152.5 2.4 %exponential_reduce_fusion.4 = f32[16,32,16]{1,2,0:T(8,128)S(1)} fusion(bf16[16,128,128]{2,1,0:T(8,128)(2,1)} %get-tuple-element.78, bf16[16,16,32,128]{3,2,1,0:T(8,128)(2,1)S(1)} %get-tuple-element.77, s32[]{:T(128)} %get-tuple-element.70), kind=kOutput, calls=%fused_computation.2.clone.1 | convolution fusion | flops 270524416 | bytes 688132 | tf_op jit(solution)/shard_map/while/body/eval_jaxpr/sie,pje->sipj/dot_general | solution.py:22
  154.9 0.1 multiply_reduce_fusion.4
  155.0 0.6 bitcast_dynamic-update-slice_fusion.2
  155.6 2.4 %exponential_reduce_fusion.4 = f32[16,32,16]{1,2,0:T(8,128)S(1)} fusion(bf16[16,128,128]{2,1,0:T(8,128)(2,1)} %get-tuple-element.78, bf16[16,16,32,128]{3,2,1,0:T(8,128)(2,1)S(1)} %get-tuple-element.77, s32[]{:T(128)} %get-tuple-element.70), kind=kOutput, calls=%fused_computation.2.clone.1 | convolution fusion | flops 270524416 | bytes 688132 | tf_op jit(solution)/shard_map/while/body/eval_jaxpr/sie,pje->sipj/dot_general | solution.py:22
  158.0 0.1 multiply_reduce_fusion.4
  158.1 0.6 bitcast_dynamic-update-slice_fusion.2
  158.7 2.4 %exponential_reduce_fusion.4 = f32[16,32,16]{1,2,0:T(8,128)S(1)} fusion(bf16[16,128,128]{2,1,0:T(8,128)(2,1)} %get-tuple-element.78, bf16[16,16,32,128]{3,2,1,0:T(8,128)(2,1)S(1)} %get-tuple-element.77, s32[]{:T(128)} %get-tuple-element.70), kind=kOutput, calls=%fused_computation.2.clone.1 | convolution fusion | flops 270524416 | bytes 688132 | tf_op jit(solution)/shard_map/while/body/eval_jaxpr/sie,pje->sipj/dot_general | solution.py:22
  161.2 0.6 bitcast_dynamic-update-slice_fusion.2
  161.8 2.4 %exponential_reduce_fusion.4 = f32[16,32,16]{1,2,0:T(8,128)S(1)} fusion(bf16[16,128,128]{2,1,0:T(8,128)(2,1)} %get-tuple-element.78, bf16[16,16,32,128]{3,2,1,0:T(8,128)(2,1)S(1)} %get-tuple-element.77, s32[]{:T(128)} %get-tuple-element.70), kind=kOutput, calls=%fused_computation.2.clone.1 | convolution fusion | flops 270524416 | bytes 688132 | tf_op jit(solution)/shard_map/while/body/eval_jaxpr/sie,pje->sipj/dot_general | solution.py:22
  164.3 0.6 bitcast_dynamic-update-slice_fusion.2
  164.9 2.4 %exponential_reduce_fusion.4 = f32[16,32,16]{1,2,0:T(8,128)S(1)} fusion(bf16[16,128,128]{2,1,0:T(8,128)(2,1)} %get-tuple-element.78, bf16[16,16,32,128]{3,2,1,0:T(8,128)(2,1)S(1)} %get-tuple-element.77, s32[]{:T(128)} %get-tuple-element.70), kind=kOutput, calls=%fused_computation.2.clone.1 | convolution fusion | flops 270524416 | bytes 688132 | tf_op jit(solution)/shard_map/while/body/eval_jaxpr/sie,pje->sipj/dot_general | solution.py:22
  167.4 0.6 bitcast_dynamic-update-slice_fusion.2
  168.0 2.4 %exponential_reduce_fusion.4 = f32[16,32,16]{1,2,0:T(8,128)S(1)} fusion(bf16[16,128,128]{2,1,0:T(8,128)(2,1)} %get-tuple-element.78, bf16[16,16,32,128]{3,2,1,0:T(8,128)(2,1)S(1)} %get-tuple-element.77, s32[]{:T(128)} %get-tuple-element.70), kind=kOutput, calls=%fused_computation.2.clone.1 | convolution fusion | flops 270524416 | bytes 688132 | tf_op jit(solution)/shard_map/while/body/eval_jaxpr/sie,pje->sipj/dot_general | solution.py:22
  170.5 0.6 bitcast_dynamic-update-slice_fusion.2
  171.1 2.4 %exponential_reduce_fusion.4 = f32[16,32,16]{1,2,0:T(8,128)S(1)} fusion(bf16[16,128,128]{2,1,0:T(8,128)(2,1)} %get-tuple-element.78, bf16[16,16,32,128]{3,2,1,0:T(8,128)(2,1)S(1)} %get-tuple-element.77, s32[]{:T(128)} %get-tuple-element.70), kind=kOutput, calls=%fused_computation.2.clone.1 | convolution fusion | flops 270524416 | bytes 688132 | tf_op jit(solution)/shard_map/while/body/eval_jaxpr/sie,pje->sipj/dot_general | solution.py:22
  173.6 0.6 bitcast_dynamic-update-slice_fusion.2
  174.2 2.4 %exponential_reduce_fusion.4 = f32[16,32,16]{1,2,0:T(8,128)S(1)} fusion(bf16[16,128,128]{2,1,0:T(8,128)(2,1)} %get-tuple-element.78, bf16[16,16,32,128]{3,2,1,0:T(8,128)(2,1)S(1)} %get-tuple-element.77, s32[]{:T(128)} %get-tuple-element.70), kind=kOutput, calls=%fused_computation.2.clone.1 | convolution fusion | flops 270524416 | bytes 688132 | tf_op jit(solution)/shard_map/while/body/eval_jaxpr/sie,pje->sipj/dot_general | solution.py:22
  176.6 0.1 multiply_reduce_fusion.4
  176.8 0.6 bitcast_dynamic-update-slice_fusion.2
  177.4 2.4 %exponential_reduce_fusion.4 = f32[16,32,16]{1,2,0:T(8,128)S(1)} fusion(bf16[16,128,128]{2,1,0:T(8,128)(2,1)} %get-tuple-element.78, bf16[16,16,32,128]{3,2,1,0:T(8,128)(2,1)S(1)} %get-tuple-element.77, s32[]{:T(128)} %get-tuple-element.70), kind=kOutput, calls=%fused_computation.2.clone.1 | convolution fusion | flops 270524416 | bytes 688132 | tf_op jit(solution)/shard_map/while/body/eval_jaxpr/sie,pje->sipj/dot_general | solution.py:22
  179.9 0.6 bitcast_dynamic-update-slice_fusion.2
  180.5 2.4 %exponential_reduce_fusion.4 = f32[16,32,16]{1,2,0:T(8,128)S(1)} fusion(bf16[16,128,128]{2,1,0:T(8,128)(2,1)} %get-tuple-element.78, bf16[16,16,32,128]{3,2,1,0:T(8,128)(2,1)S(1)} %get-tuple-element.77, s32[]{:T(128)} %get-tuple-element.70), kind=kOutput, calls=%fused_computation.2.clone.1 | convolution fusion | flops 270524416 | bytes 688132 | tf_op jit(solution)/shard_map/while/body/eval_jaxpr/sie,pje->sipj/dot_general | solution.py:22
  182.9 0.1 multiply_reduce_fusion.4
  183.0 0.6 bitcast_dynamic-update-slice_fusion.2
  183.6 2.4 %exponential_reduce_fusion.4 = f32[16,32,16]{1,2,0:T(8,128)S(1)} fusion(bf16[16,128,128]{2,1,0:T(8,128)(2,1)} %get-tuple-element.78, bf16[16,16,32,128]{3,2,1,0:T(8,128)(2,1)S(1)} %get-tuple-element.77, s32[]{:T(128)} %get-tuple-element.70), kind=kOutput, calls=%fused_computation.2.clone.1 | convolution fusion | flops 270524416 | bytes 688132 | tf_op jit(solution)/shard_map/while/body/eval_jaxpr/sie,pje->sipj/dot_general | solution.py:22
  186.1 0.6 bitcast_dynamic-update-slice_fusion.2
  186.7 2.4 %exponential_reduce_fusion.4 = f32[16,32,16]{1,2,0:T(8,128)S(1)} fusion(bf16[16,128,128]{2,1,0:T(8,128)(2,1)} %get-tuple-element.78, bf16[16,16,32,128]{3,2,1,0:T(8,128)(2,1)S(1)} %get-tuple-element.77, s32[]{:T(128)} %get-tuple-element.70), kind=kOutput, calls=%fused_computation.2.clone.1 | convolution fusion | flops 270524416 | bytes 688132 | tf_op jit(solution)/shard_map/while/body/eval_jaxpr/sie,pje->sipj/dot_general | solution.py:22
  189.2 0.6 bitcast_dynamic-update-slice_fusion.2
  189.8 7.5 %all-to-all-start.1 = ((f32[128,2,16]{2,1,0:T(2,128)}), f32[128,2,16]{2,1,0:T(2,128)S(1)}, u32[]{:S(2)}, u32[]{:S(2)}) async-start(f32[128,2,16]{2,1,0:T(2,128)} %bitcast.10), calls=%async_computation.1 | async-start | bytes 262144 | tf_op jit(solution)/shard_map/all_to_all | solution.py:65
  197.3 11.9 %all-to-all-done.1 = f32[128,2,16]{2,1,0:T(2,128)S(1)} async-done(((f32[128,2,16]{2,1,0:T(2,128)}), f32[128,2,16]{2,1,0:T(2,128)S(1)}, u32[]{:S(2)}, u32[]{:S(2)}) %all-to-all-start.1) | async-done | bytes 16416 | tf_op jit(solution)/shard_map/all_to_all | solution.py:65
  209.2 0.6 gather_fusion.1
  209.9 12.0 %all_gather.3 = f32[32,4,64]{0,1,2:T(4,128)S(1)} all-gather(f32[32,4,16]{0,1,2:T(4,128)S(1)} %copy.21), channel_id=1, replica_groups=mesh['dp'=128,'mp'=4] {'mp'}, dimensions={2}, use_global_device_ids=true | all-gather | bytes 40960 | tf_op jit(solution)/shard_map/all_gather | solution.py:68
  222.1 0.2 multiply_reduce_fusion.2
  222.3 0.5 log_add_fusion
  (35 shorter events, 1.7 us)
Async XLA Ops:
  6.5 1.0 copy-start
  6.5 61.6 %all-reduce.2.cloned.1.call-start = ((), (), s32[]{:S(2)}) async-start(), calls=%async_computation.2 | async-start | bytes 1048576 | tf_op jit(solution)/shard_map/psum | solution.py:56
  73.4 14.3 %copy-start.3 = (s32[32,4]{0,1:T(4,128)S(1)}, s32[32,4]{0,1:T(4,128)}, u32[]{:S(2)}) copy-start(s32[32,4]{0,1:T(4,128)} %param.11) | copy-start | bytes 1540
  73.4 14.5 %copy-start.2 = (f32[32,4,64]{2,1,0:T(4,128)S(1)}, f32[32,4,64]{2,1,0:T(4,128)}, u32[]{:S(2)}) copy-start(f32[32,4,64]{2,1,0:T(4,128)} %param.10) | copy-start | bytes 98308
  73.4 14.9 %copy-start.1 = (bf16[16,128,128]{2,1,0:T(8,128)(2,1)S(1)}, bf16[16,128,128]{2,1,0:T(8,128)(2,1)}, u32[]{:S(2)}) copy-start(bf16[16,128,128]{2,1,0:T(8,128)(2,1)} %param.9) | copy-start | bytes 1572868
  73.4 66.7 %all-to-all-start = ((bf16[128,2,32,128]{3,2,1,0:T(8,128)(2,1)}), bf16[128,2,32,128]{3,2,1,0:T(8,128)(2,1)S(1)}, u32[]{:S(2)}, u32[]{:S(2)}) async-start(bf16[128,2,32,128]{3,2,1,0:T(8,128)(2,1)} %broadcast_multiply_fusion), calls=%async_computation | async-start | bytes 4194304 | tf_op jit(solution)/shard_map/all_to_all | solution.py:61
  189.8 19.4 %all-to-all-start.1 = ((f32[128,2,16]{2,1,0:T(2,128)}), f32[128,2,16]{2,1,0:T(2,128)S(1)}, u32[]{:S(2)}, u32[]{:S(2)}) async-start(f32[128,2,16]{2,1,0:T(2,128)} %bitcast.10), calls=%async_computation.1 | async-start | bytes 262144 | tf_op jit(solution)/shard_map/all_to_all | solution.py:65
Sparse Core Ops, SparseCore 0:
  9.7 58.4 all-reduce.1
where the time goes:
time: 231 us; the launch traced here: 230 us
  waiting for transfers between devices  119 us (52%)
  matrix products  39.9 us (17%)
  starting transfers between devices  21.8 us (9%)
  local copies, waits for them, and re-layouts  13.7 us (6%)
  between operations  13.6 us (6%)
  blocking collectives  12 us (5%)
  other arithmetic  9.3 us (4%)
    psum x1, waiting for transfers between devices, per_device(): projected = lax.psum(partial_sum, 'mp')  57 us
    all_to_all x1, waiting for transfers between devices, per_device(): lax.all_to_all(outgoing, 'dp', split_axis=0, concat_axis=0, tiled=True)  50.3 us
    dot_general x16, matrix products, block_scores(): jnp.einsum('sie,pje->sipj', slot_block, passage_vecs, preferred_element_t...  38 us
    all_to_all x1, starting transfers between devices, per_device(): lax.all_to_all(outgoing, 'dp', split_axis=0, concat_axis=0, tiled=True)  14.3 us
    all_gather x1, blocking collectives, per_device(): student = lax.all_gather(home_scores, 'mp', axis=2, tiled=True)  12 us
    all_to_all x1, waiting for transfers between devices, per_device(): lax.all_to_all(scores, 'dp', split_axis=0, concat_axis=0, tiled=True)  11.9 us
    dynamic_update_slice x16, local copies, waits for them, and re-layouts, soft_scores(): scored = lax.map(block_scores, blocked)  9.63 us
    all_to_all x1, starting transfers between devices, per_device(): lax.all_to_all(scores, 'dp', split_axis=0, concat_axis=0, tiled=True)  7.48 us
  transfers between devices with their start and end apart: 3, of which 3 were waited for; matrix products, arithmetic and copies ran while one was open for 2% of the time, Pallas kernels for 0%

commit v1 on v0

--- a/solution.py
+++ b/solution.py
@@ -53,7 +53,11 @@
     row_query = jnp.arange(row_count, dtype=jnp.int32) // pick_count
     source = jnp.sum(matches * row_query[None, :], axis=1)
     filled = jnp.sum(matches, axis=1)
-    projected = lax.psum(partial_sum, "mp")
+    projected = partial_sum
+    for hop in (1, 2):
+        projected = projected + lax.ppermute(
+            projected, "mp", [(dev, dev ^ hop) for dev in range(4)]
+        )
     query_vecs = unit_rows(projected).astype(jnp.bfloat16)
     tokens = query_vecs.shape[1]
     outgoing = query_vecs[source] * filled[:, None, None].astype(jnp.bfloat16)

time: 231 us -> 192 us (0.83)
  the two profiles are of different devices: /device:TPU:8 before, /device:TPU:2 now
where the time goes in v1:
time: 192 us; the launch traced here: 191 us
  waiting for transfers between devices  79.7 us (42%)
  matrix products  39.1 us (20%)
  starting transfers between devices  38.4 us (20%)
  local copies, waits for them, and re-layouts  13.7 us (7%)
  blocking collectives  12 us (6%)
  other arithmetic  7.3 us (4%)
    all_to_all x1, waiting for transfers between devices, per_device(): lax.all_to_all(outgoing, 'dp', split_axis=0, concat_axis=0, tiled=True)  50.3 us
    dot_general x16, matrix products, block_scores(): jnp.einsum('sie,pje->sipj', slot_block, passage_vecs, preferred_element_t...  38 us
    all_to_all x1, starting transfers between devices, per_device(): lax.all_to_all(outgoing, 'dp', split_axis=0, concat_axis=0, tiled=True)  19.1 us
    ppermute x2, waiting for transfers between devices, per_device(): lax.ppermute(projected, 'mp', [(dev, dev ^ hop) for dev in range(4)])  17.1 us
    all_to_all x1, waiting for transfers between devices, per_device(): lax.all_to_all(scores, 'dp', split_axis=0, concat_axis=0, tiled=True)  12.3 us
    all_gather x1, blocking collectives, per_device(): student = lax.all_gather(home_scores, 'mp', axis=2, tiled=True)  12 us
    ppermute x2, starting transfers between devices, per_device(): lax.ppermute(projected, 'mp', [(dev, dev ^ hop) for dev in range(4)])  11.8 us
    dynamic_update_slice x16, local copies, waits for them, and re-layouts, soft_scores(): scored = lax.map(block_scores, blocked)  9.63 us
  transfers between devices with their start and end apart: 4, of which 4 were waited for; matrix products, arithmetic and copies ran while one was open for 2% of the time, Pallas kernels for 0%

profile of v1, /device:TPU:2, one launch (start us, length us, event | category | flops | bytes accessed | tf_op | source)
XLA Modules:
  0.0 190.6 jit_solution(9149132172182549748)
XLA Ops:
  0.0 1.0 copy-done
  1.0 1.1 fusion.7
  2.1 7.8 %collective-permute-start = (f32[32,32,128]{2,1,0:T(8,128)S(1)}, f32[32,32,128]{2,1,0:T(8,128)S(1)}, u32[]{:S(2)}, u32[]{:S(2)}) collective-permute-start(f32[32,32,128]{2,1,0:T(8,128)S(1)} %fusion.7), channel_id=1, source_target_pairs={{0,1},{1,0},{2,3},{3,2},{4,5},{5,4},{6,7},{7,6},{8,9},{9,8},{10,11... | collective-permute-start | bytes 1572872 | tf_op jit(solution)/shard_map/ppermute | solution.py:58
  9.9 0.8 copy.19
  10.9 0.2 reduce_window_sum.11
  11.1 0.2 select_reduce_fusion.1
  11.2 6.5 %collective-permute-done = f32[32,32,128]{2,1,0:T(8,128)S(1)} collective-permute-done((f32[32,32,128]{2,1,0:T(8,128)S(1)}, f32[32,32,128]{2,1,0:T(8,128)S(1)}, u32[]{:S(2)}, u32[]{:S(2)}) %collective-permute-start) | collective-permute-done | bytes 524320 | tf_op jit(solution)/shard_map/ppermute | solution.py:58
  17.8 4.0 %collective-permute-start.1 = (f32[32,32,128]{2,1,0:T(8,128)S(1)}, f32[32,32,128]{2,1,0:T(8,128)S(1)}, u32[]{:S(2)}, u32[]{:S(2)}) collective-permute-start(f32[32,32,128]{2,1,0:T(8,128)S(1)} %add.81), channel_id=1, source_target_pairs={{0,2},{1,3},{2,0},{3,1},{4,6},{5,7},{6,4},{7,5},{8,10},{9,11},{10,... | collective-permute-start | bytes 1572872 | tf_op jit(solution)/shard_map/ppermute | solution.py:58
  21.8 0.2 convert_reduce_fusion
  22.0 0.2 convert_element_type.30
  22.2 10.7 %collective-permute-done.1 = f32[32,32,128]{2,1,0:T(8,128)S(1)} collective-permute-done((f32[32,32,128]{2,1,0:T(8,128)S(1)}, f32[32,32,128]{2,1,0:T(8,128)S(1)}, u32[]{:S(2)}, u32[]{:S(2)}) %collective-permute-start.1) | collective-permute-done | bytes 524320 | tf_op jit(solution)/shard_map/ppermute | solution.py:58
  32.8 0.2 multiply_reduce_fusion.1
  33.1 0.2 multiply_convert_fusion
  33.3 1.0 gather_fusion
  34.3 1.7 broadcast_multiply_fusion
  36.0 19.1 %all-to-all-start = ((bf16[128,2,32,128]{3,2,1,0:T(8,128)(2,1)}), bf16[128,2,32,128]{3,2,1,0:T(8,128)(2,1)S(1)}, u32[]{:S(2)}, u32[]{:S(2)}) async-start(bf16[128,2,32,128]{3,2,1,0:T(8,128)(2,1)} %broadcast_multiply_fusion), calls=%async_computation | async-start | bytes 4194304 | tf_op jit(solution)/shard_map/all_to_all | solution.py:65
  55.3 0.3 exponential_reduce_fusion.2
  55.6 0.3 fusion.4
  56.0 1.1 fusion.5
  57.1 50.3 %all-to-all-done = bf16[128,2,32,128]{3,2,1,0:T(8,128)(2,1)S(1)} async-done(((bf16[128,2,32,128]{3,2,1,0:T(8,128)(2,1)}), bf16[128,2,32,128]{3,2,1,0:T(8,128)(2,1)S(1)}, u32[]{:S(2)}, u32[]{:S(2)}) %all-to-all-start) | async-done | bytes 2097184 | tf_op jit(solution)/shard_map/all_to_all | solution.py:65
  107.4 49.7 %while.10 = (s32[]{:T(128)}, f32[16,16,16]{2,1,0:T(8,128)}, bf16[16,16,32,128]{3,2,1,0:T(8,128)(2,1)S(1)}, bf16[16,128,128]{2,1,0:T(8,128)(2,1)}, s32[]{:T(128)}) while((s32[]{:T(128)}, f32[16,16,16]{2,1,0:T(8,128)}, bf16[16,16,32,128]{3,2,1,0:T(8,128)(2,1)S(1)}, bf16[16,128,128]{2,1,0:T(8,128)(2,1)}, s32[]{:T(128)}) %tuple.24), condition=%wide.region_10.11_spmd, body=%wide.region_7.10_spmd.sunk | while | flops 270540544 | bytes 731713 | solution.py:28
  107.4 2.4 %exponential_reduce_fusion.4 = f32[16,32,16]{1,2,0:T(8,128)S(1)} fusion(bf16[16,128,128]{2,1,0:T(8,128)(2,1)} %get-tuple-element.80, bf16[16,16,32,128]{3,2,1,0:T(8,128)(2,1)S(1)} %get-tuple-element.79, s32[]{:T(128)} %get-tuple-element.72), kind=kOutput, calls=%fused_computation.2.clone.1 | convolution fusion | flops 270524416 | bytes 688132 | tf_op jit(solution)/shard_map/while/body/eval_jaxpr/sie,pje->sipj/dot_general | solution.py:22
  109.8 0.1 multiply_reduce_fusion.4
  109.9 0.6 bitcast_dynamic-update-slice_fusion.2
  110.5 2.4 %exponential_reduce_fusion.4 = f32[16,32,16]{1,2,0:T(8,128)S(1)} fusion(bf16[16,128,128]{2,1,0:T(8,128)(2,1)} %get-tuple-element.80, bf16[16,16,32,128]{3,2,1,0:T(8,128)(2,1)S(1)} %get-tuple-element.79, s32[]{:T(128)} %get-tuple-element.72), kind=kOutput, calls=%fused_computation.2.clone.1 | convolution fusion | flops 270524416 | bytes 688132 | tf_op jit(solution)/shard_map/while/body/eval_jaxpr/sie,pje->sipj/dot_general | solution.py:22
  112.9 0.1 multiply_reduce_fusion.4
  113.0 0.6 bitcast_dynamic-update-slice_fusion.2
  113.6 2.4 %exponential_reduce_fusion.4 = f32[16,32,16]{1,2,0:T(8,128)S(1)} fusion(bf16[16,128,128]{2,1,0:T(8,128)(2,1)} %get-tuple-element.80, bf16[16,16,32,128]{3,2,1,0:T(8,128)(2,1)S(1)} %get-tuple-element.79, s32[]{:T(128)} %get-tuple-element.72), kind=kOutput, calls=%fused_computation.2.clone.1 | convolution fusion | flops 270524416 | bytes 688132 | tf_op jit(solution)/shard_map/while/body/eval_jaxpr/sie,pje->sipj/dot_general | solution.py:22
  116.0 0.1 multiply_reduce_fusion.4
  116.1 0.6 bitcast_dynamic-update-slice_fusion.2
  116.7 2.4 %exponential_reduce_fusion.4 = f32[16,32,16]{1,2,0:T(8,128)S(1)} fusion(bf16[16,128,128]{2,1,0:T(8,128)(2,1)} %get-tuple-element.80, bf16[16,16,32,128]{3,2,1,0:T(8,128)(2,1)S(1)} %get-tuple-element.79, s32[]{:T(128)} %get-tuple-element.72), kind=kOutput, calls=%fused_computation.2.clone.1 | convolution fusion | flops 270524416 | bytes 688132 | tf_op jit(solution)/shard_map/while/body/eval_jaxpr/sie,pje->sipj/dot_general | solution.py:22
  119.2 0.6 bitcast_dynamic-update-slice_fusion.2
  119.8 2.4 %exponential_reduce_fusion.4 = f32[16,32,16]{1,2,0:T(8,128)S(1)} fusion(bf16[16,128,128]{2,1,0:T(8,128)(2,1)} %get-tuple-element.80, bf16[16,16,32,128]{3,2,1,0:T(8,128)(2,1)S(1)} %get-tuple-element.79, s32[]{:T(128)} %get-tuple-element.72), kind=kOutput, calls=%fused_computation.2.clone.1 | convolution fusion | flops 270524416 | bytes 688132 | tf_op jit(solution)/shard_map/while/body/eval_jaxpr/sie,pje->sipj/dot_general | solution.py:22
  122.3 0.6 bitcast_dynamic-update-slice_fusion.2
  122.9 2.4 %exponential_reduce_fusion.4 = f32[16,32,16]{1,2,0:T(8,128)S(1)} fusion(bf16[16,128,128]{2,1,0:T(8,128)(2,1)} %get-tuple-element.80, bf16[16,16,32,128]{3,2,1,0:T(8,128)(2,1)S(1)} %get-tuple-element.79, s32[]{:T(128)} %get-tuple-element.72), kind=kOutput, calls=%fused_computation.2.clone.1 | convolution fusion | flops 270524416 | bytes 688132 | tf_op jit(solution)/shard_map/while/body/eval_jaxpr/sie,pje->sipj/dot_general | solution.py:22
  125.4 0.6 bitcast_dynamic-update-slice_fusion.2
  126.0 2.4 %exponential_reduce_fusion.4 = f32[16,32,16]{1,2,0:T(8,128)S(1)} fusion(bf16[16,128,128]{2,1,0:T(8,128)(2,1)} %get-tuple-element.80, bf16[16,16,32,128]{3,2,1,0:T(8,128)(2,1)S(1)} %get-tuple-element.79, s32[]{:T(128)} %get-tuple-element.72), kind=kOutput, calls=%fused_computation.2.clone.1 | convolution fusion | flops 270524416 | bytes 688132 | tf_op jit(solution)/shard_map/while/body/eval_jaxpr/sie,pje->sipj/dot_general | solution.py:22
  128.5 0.6 bitcast_dynamic-update-slice_fusion.2
  129.2 2.4 %exponential_reduce_fusion.4 = f32[16,32,16]{1,2,0:T(8,128)S(1)} fusion(bf16[16,128,128]{2,1,0:T(8,128)(2,1)} %get-tuple-element.80, bf16[16,16,32,128]{3,2,1,0:T(8,128)(2,1)S(1)} %get-tuple-element.79, s32[]{:T(128)} %get-tuple-element.72), kind=kOutput, calls=%fused_computation.2.clone.1 | convolution fusion | flops 270524416 | bytes 688132 | tf_op jit(solution)/shard_map/while/body/eval_jaxpr/sie,pje->sipj/dot_general | solution.py:22
  131.7 0.6 bitcast_dynamic-update-slice_fusion.2
  132.3 2.4 %exponential_reduce_fusion.4 = f32[16,32,16]{1,2,0:T(8,128)S(1)} fusion(bf16[16,128,128]{2,1,0:T(8,128)(2,1)} %get-tuple-element.80, bf16[16,16,32,128]{3,2,1,0:T(8,128)(2,1)S(1)} %get-tuple-element.79, s32[]{:T(128)} %get-tuple-element.72), kind=kOutput, calls=%fused_computation.2.clone.1 | convolution fusion | flops 270524416 | bytes 688132 | tf_op jit(solution)/shard_map/while/body/eval_jaxpr/sie,pje->sipj/dot_general | solution.py:22
  134.6 0.1 multiply_reduce_fusion.4
  134.8 0.6 bitcast_dynamic-update-slice_fusion.2
  135.4 2.4 %exponential_reduce_fusion.4 = f32[16,32,16]{1,2,0:T(8,128)S(1)} fusion(bf16[16,128,128]{2,1,0:T(8,128)(2,1)} %get-tuple-element.80, bf16[16,16,32,128]{3,2,1,0:T(8,128)(2,1)S(1)} %get-tuple-element.79, s32[]{:T(128)} %get-tuple-element.72), kind=kOutput, calls=%fused_computation.2.clone.1 | convolution fusion | flops 270524416 | bytes 688132 | tf_op jit(solution)/shard_map/while/body/eval_jaxpr/sie,pje->sipj/dot_general | solution.py:22
  137.9 0.6 bitcast_dynamic-update-slice_fusion.2
  138.5 2.4 %exponential_reduce_fusion.4 = f32[16,32,16]{1,2,0:T(8,128)S(1)} fusion(bf16[16,128,128]{2,1,0:T(8,128)(2,1)} %get-tuple-element.80, bf16[16,16,32,128]{3,2,1,0:T(8,128)(2,1)S(1)} %get-tuple-element.79, s32[]{:T(128)} %get-tuple-element.72), kind=kOutput, calls=%fused_computation.2.clone.1 | convolution fusion | flops 270524416 | bytes 688132 | tf_op jit(solution)/shard_map/while/body/eval_jaxpr/sie,pje->sipj/dot_general | solution.py:22
  141.0 0.6 bitcast_dynamic-update-slice_fusion.2
  141.6 2.4 %exponential_reduce_fusion.4 = f32[16,32,16]{1,2,0:T(8,128)S(1)} fusion(bf16[16,128,128]{2,1,0:T(8,128)(2,1)} %get-tuple-element.80, bf16[16,16,32,128]{3,2,1,0:T(8,128)(2,1)S(1)} %get-tuple-element.79, s32[]{:T(128)} %get-tuple-element.72), kind=kOutput, calls=%fused_computation.2.clone.1 | convolution fusion | flops 270524416 | bytes 688132 | tf_op jit(solution)/shard_map/while/body/eval_jaxpr/sie,pje->sipj/dot_general | solution.py:22
  144.1 0.6 bitcast_dynamic-update-slice_fusion.2
  144.7 2.4 %exponential_reduce_fusion.4 = f32[16,32,16]{1,2,0:T(8,128)S(1)} fusion(bf16[16,128,128]{2,1,0:T(8,128)(2,1)} %get-tuple-element.80, bf16[16,16,32,128]{3,2,1,0:T(8,128)(2,1)S(1)} %get-tuple-element.79, s32[]{:T(128)} %get-tuple-element.72), kind=kOutput, calls=%fused_computation.2.clone.1 | convolution fusion | flops 270524416 | bytes 688132 | tf_op jit(solution)/shard_map/while/body/eval_jaxpr/sie,pje->sipj/dot_general | solution.py:22
  147.2 0.6 bitcast_dynamic-update-slice_fusion.2
  147.8 2.4 %exponential_reduce_fusion.4 = f32[16,32,16]{1,2,0:T(8,128)S(1)} fusion(bf16[16,128,128]{2,1,0:T(8,128)(2,1)} %get-tuple-element.80, bf16[16,16,32,128]{3,2,1,0:T(8,128)(2,1)S(1)} %get-tuple-element.79, s32[]{:T(128)} %get-tuple-element.72), kind=kOutput, calls=%fused_computation.2.clone.1 | convolution fusion | flops 270524416 | bytes 688132 | tf_op jit(solution)/shard_map/while/body/eval_jaxpr/sie,pje->sipj/dot_general | solution.py:22
  150.3 0.6 bitcast_dynamic-update-slice_fusion.2
  150.9 2.4 %exponential_reduce_fusion.4 = f32[16,32,16]{1,2,0:T(8,128)S(1)} fusion(bf16[16,128,128]{2,1,0:T(8,128)(2,1)} %get-tuple-element.80, bf16[16,16,32,128]{3,2,1,0:T(8,128)(2,1)S(1)} %get-tuple-element.79, s32[]{:T(128)} %get-tuple-element.72), kind=kOutput, calls=%fused_computation.2.clone.1 | convolution fusion | flops 270524416 | bytes 688132 | tf_op jit(solution)/shard_map/while/body/eval_jaxpr/sie,pje->sipj/dot_general | solution.py:22
  153.4 0.6 bitcast_dynamic-update-slice_fusion.2
  154.0 2.4 %exponential_reduce_fusion.4 = f32[16,32,16]{1,2,0:T(8,128)S(1)} fusion(bf16[16,128,128]{2,1,0:T(8,128)(2,1)} %get-tuple-element.80, bf16[16,16,32,128]{3,2,1,0:T(8,128)(2,1)S(1)} %get-tuple-element.79, s32[]{:T(128)} %get-tuple-element.72), kind=kOutput, calls=%fused_computation.2.clone.1 | convolution fusion | flops 270524416 | bytes 688132 | tf_op jit(solution)/shard_map/while/body/eval_jaxpr/sie,pje->sipj/dot_general | solution.py:22
  156.4 0.1 multiply_reduce_fusion.4
  156.5 0.6 bitcast_dynamic-update-slice_fusion.2
  157.1 7.5 %all-to-all-start.1 = ((f32[128,2,16]{2,1,0:T(2,128)}), f32[128,2,16]{2,1,0:T(2,128)S(1)}, u32[]{:S(2)}, u32[]{:S(2)}) async-start(f32[128,2,16]{2,1,0:T(2,128)} %bitcast.10), calls=%async_computation.1 | async-start | bytes 262144 | tf_op jit(solution)/shard_map/all_to_all | solution.py:69
  164.7 12.3 %all-to-all-done.1 = f32[128,2,16]{2,1,0:T(2,128)S(1)} async-done(((f32[128,2,16]{2,1,0:T(2,128)}), f32[128,2,16]{2,1,0:T(2,128)S(1)}, u32[]{:S(2)}, u32[]{:S(2)}) %all-to-all-start.1) | async-done | bytes 16416 | tf_op jit(solution)/shard_map/all_to_all | solution.py:69
  177.0 0.6 gather_fusion.1
  177.7 12.0 %all_gather.3 = f32[32,4,64]{0,1,2:T(4,128)S(1)} all-gather(f32[32,4,16]{0,1,2:T(4,128)S(1)} %copy.21), channel_id=1, replica_groups=mesh['dp'=128,'mp'=4] {'mp'}, dimensions={2}, use_global_device_ids=true | all-gather | bytes 40960 | tf_op jit(solution)/shard_map/all_gather | solution.py:72
  189.9 0.2 multiply_reduce_fusion.2
  190.1 0.5 log_add_fusion
  (37 shorter events, 2.1 us)
Async XLA Ops:
  0.0 1.0 copy-start
  2.1 15.6 %collective-permute-start = (f32[32,32,128]{2,1,0:T(8,128)S(1)}, f32[32,32,128]{2,1,0:T(8,128)S(1)}, u32[]{:S(2)}, u32[]{:S(2)}) collective-permute-start(f32[32,32,128]{2,1,0:T(8,128)S(1)} %fusion.7), channel_id=1, source_target_pairs={{0,1},{1,0},{2,3},{3,2},{4,5},{5,4},{6,7},{7,6},{8,9},{9,8},{10,11... | collective-permute-start | bytes 1572872 | tf_op jit(solution)/shard_map/ppermute | solution.py:58
  17.8 15.1 %collective-permute-start.1 = (f32[32,32,128]{2,1,0:T(8,128)S(1)}, f32[32,32,128]{2,1,0:T(8,128)S(1)}, u32[]{:S(2)}, u32[]{:S(2)}) collective-permute-start(f32[32,32,128]{2,1,0:T(8,128)S(1)} %add.81), channel_id=1, source_target_pairs={{0,2},{1,3},{2,0},{3,1},{4,6},{5,7},{6,4},{7,5},{8,10},{9,11},{10,... | collective-permute-start | bytes 1572872 | tf_op jit(solution)/shard_map/ppermute | solution.py:58
  36.0 19.1 %copy-start.3 = (s32[32,4]{0,1:T(4,128)S(1)}, s32[32,4]{0,1:T(4,128)}, u32[]{:S(2)}) copy-start(s32[32,4]{0,1:T(4,128)} %param.11) | copy-start | bytes 1540
  36.0 19.3 %copy-start.2 = (f32[32,4,64]{2,1,0:T(4,128)S(1)}, f32[32,4,64]{2,1,0:T(4,128)}, u32[]{:S(2)}) copy-start(f32[32,4,64]{2,1,0:T(4,128)} %param.10) | copy-start | bytes 98308
  36.0 19.6 %copy-start.1 = (bf16[16,128,128]{2,1,0:T(8,128)(2,1)S(1)}, bf16[16,128,128]{2,1,0:T(8,128)(2,1)}, u32[]{:S(2)}) copy-start(bf16[16,128,128]{2,1,0:T(8,128)(2,1)} %param.9) | copy-start | bytes 1572868
  36.0 71.4 %all-to-all-start = ((bf16[128,2,32,128]{3,2,1,0:T(8,128)(2,1)}), bf16[128,2,32,128]{3,2,1,0:T(8,128)(2,1)S(1)}, u32[]{:S(2)}, u32[]{:S(2)}) async-start(bf16[128,2,32,128]{3,2,1,0:T(8,128)(2,1)} %broadcast_multiply_fusion), calls=%async_computation | async-start | bytes 4194304 | tf_op jit(solution)/shard_map/all_to_all | solution.py:65
  157.1 19.8 %all-to-all-start.1 = ((f32[128,2,16]{2,1,0:T(2,128)}), f32[128,2,16]{2,1,0:T(2,128)S(1)}, u32[]{:S(2)}, u32[]{:S(2)}) async-start(f32[128,2,16]{2,1,0:T(2,128)} %bitcast.10), calls=%async_computation.1 | async-start | bytes 262144 | tf_op jit(solution)/shard_map/all_to_all | solution.py:69
